TPU v7x, 256 devices: a whole 4x4x8 slice. The times are simulated.
256 devices in a mesh: comp: 16 (over z, core), blk: 16 (over x, y).
Axes of the slice: x: 4, y: 4, z: 8, core: 2. Of those that a mesh axis runs over, the one named last changes fastest.
Arguments:
- state_now: float32 [16, 6, 128, 32, 256], P('comp', None, 'blk'), may hold values from -5 to 5
- state_prev: float32 [16, 6, 128, 32, 256], P('comp', None, 'blk'), may hold values from -5 to 5
- viscosity: float32 [16, 128, 32, 256], P('comp', 'blk'), may hold values from 0.05 to 0.5
- jacobian: float32 [16, 3, 6, 6], P('comp'), may hold values from -0.4 to 0.4
- donor_cell: int32 [16, 16, 16, 2, 8, 128], P('comp', 'blk'), may hold values from 0 to 57343, as said below
- interp_weight: float32 [16, 16, 16, 2, 8, 128], P('comp', 'blk'), may hold values from 0 to 1
- recv_cell: int32 [16, 16, 16, 2, 128], P('comp', 'blk'), may hold values from 0 to 57343, as said below
- pair_tiles: int32 [16, 16, 16], P('blk'), may hold values from 0 to 2, as said below
Outputs:
- state_next: float32 [16, 6, 128, 32, 256], P('comp', None, 'blk')
Inputs may be any that keep to these rules, and one draw needn't show every extreme that they name: `donor_cell`: the cells of one donor tile point are the eight corners of a cube of adjacent cells, corner k = 4 i + 2 j + l offset by (i, j, l). `recv_cell`: the receiving cells of one device are all different. `pair_tiles`: for each block index some destination component takes 2 tiles from every source component.
All inputs are finite; a program needn't handle non-finite values.
Results may differ from a plain program's by a relative error of at most 0.0003.
Values sent between devices are 32-bit elements; how exact they have to be, the bound alone decides.
No kernel may reach another device: no remote copies, remote signals or barrier semaphores. Data moves between devices by JAX's collectives and lax.ppermute only.
A program may use at most 128 MiB of HBM per device.

v0:
```python
import jax
import jax.numpy as jnp
from jax import lax
from jax.sharding import PartitionSpec as P

SUBITERS = 2
time_scale = 0.5
pseudo_diag = 2.5


def padded_2(block, sides, width):
    for axis, dim in sides:
        count = lax.axis_size(axis)
        forward = [(i, i + 1) for i in range(count - 1)]
        backward = [(target, source) for source, target in forward]
        low = lax.ppermute(
            lax.slice_in_dim(block, block.shape[dim] - width, None, axis=dim), axis, forward
        )
        high = lax.ppermute(lax.slice_in_dim(block, 0, width, axis=dim), axis, backward)
        block = jnp.concatenate([low, block, high], axis=dim)
    return block


def mix(jac_dim, field):
    return jnp.einsum("vw,wxyz->vxyz", jac_dim, field, precision=lax.Precision.HIGHEST)


def flux(padded, kappa, jac):
    centre = padded[:, 1:-1]
    along_x = (padded[:, 2:] - padded[:, :-2]) * 0.5
    spread = jnp.pad(centre, ((0, 0), (0, 0), (1, 1), (1, 1)))
    along_y = (spread[:, :, 2:, 1:-1] - spread[:, :, :-2, 1:-1]) * 0.5
    along_z = (spread[:, :, 1:-1, 2:] - spread[:, :, 1:-1, :-2]) * 0.5
    beside = padded[:, 2:] + padded[:, :-2] + spread[:, :, 2:, 1:-1] + spread[:, :, :-2, 1:-1]
    beside = beside + spread[:, :, 1:-1, 2:] + spread[:, :, 1:-1, :-2]
    convect = mix(jac[0], along_x) + mix(jac[1], along_y) + mix(jac[2], along_z)
    return convect + kappa * (6.0 * centre - beside)


def relax(rstar, padded_step, kappa, diag, jac):
    centre = padded_step[:, 1:-1]
    return -(rstar + flux(padded_step, kappa, jac) - 6.0 * kappa * centre) / diag


def shards(
    state_now, state_prev, viscosity, jacobian, donor_cell, interp_weight, recv_cell, pair_tiles
):
    now = state_now[0]
    prev = state_prev[0]
    kappa = viscosity[0]
    jac = jacobian[0]
    nvar, rows, width_y, width_z = now.shape
    total_cells = rows * width_y * width_z
    comps = lax.axis_size("comp")
    mine = lax.axis_index("comp")
    slots = donor_cell.shape[3]
    tile = donor_cell.shape[5]
    diag = pseudo_diag + 6.0 * kappa
    live = lax.dynamic_index_in_dim(pair_tiles[0], mine, 1, keepdims=False)
    keep = jnp.arange(slots, dtype=jnp.int32)[None, :] < live[:, None]
    keep = jnp.broadcast_to(keep[:, :, None], (comps, slots, tile)).reshape(-1)
    cells = recv_cell[0, 0].reshape(-1)
    target_cell = jnp.where(keep, cells, total_cells)
    corner_cell = donor_cell[0, 0].reshape(-1)
    weights = interp_weight[0, 0]
    held = lax.all_to_all(weights, "comp", split_axis=0, concat_axis=0, tiled=True)
    state = now
    for sub in range(SUBITERS):
        padded = padded_2(state, (("blk", 1),), 1)
        rstar = time_scale * (3.0 * state - 4.0 * now + prev) + flux(padded, kappa, jac)
        step = -rstar / diag
        for sweep in range(2):
            padded_step = padded_2(step, (("blk", 1),), 1)
            step = relax(rstar, padded_step, kappa, diag, jac)
        state = state + step
        flat = state.reshape(nvar, total_cells)
        values = flat[:, corner_cell].reshape(nvar, comps, slots, 8, tile)
        packed = jnp.einsum("vcskp,cskp->vcsp", values, held, precision=lax.Precision.HIGHEST)
        arrived = lax.all_to_all(packed, "comp", split_axis=1, concat_axis=1, tiled=True)
        incoming = arrived.reshape(nvar, -1)
        flat = flat.at[:, target_cell].set(incoming, mode="drop")
        state = flat.reshape(nvar, rows, width_y, width_z)
    return state[None]


def solution(mesh):
    in_specs = (
        P("comp", None, "blk", None, None),
        P("comp", None, "blk", None, None),
        P("comp", "blk", None, None),
        P("comp", None, None, None),
        P("comp", "blk", None, None, None, None),
        P("comp", "blk", None, None, None, None),
        P("comp", "blk", None, None, None),
        P("blk", None, None),
    )
    out_specs = P("comp", None, "blk", None, None)
    return jax.shard_map(shards, mesh=mesh, in_specs=in_specs, out_specs=out_specs, check_vma=False)
```

profile of v0, /device:TPU:27, one launch (start us, length us, event | category | flops | bytes accessed | tf_op | source)
XLA Modules:
  0.0 560.0 jit_solution(3538027819280823225)
XLA Ops:
  0.0 9.3 %all-to-all-start = ((f32[16,2,8,128]{3,2,1,0:T(8,128)}), f32[16,2,8,128]{3,2,1,0:T(8,128)S(1)}, u32[]{:S(2)}, u32[]{:S(2)}) async-start(f32[16,2,8,128]{3,2,1,0:T(8,128)} %bitcast.167), calls=%async_computation | async-start | bytes 262144 | tf_op jit(solution)/shard_map/all_to_all | solution.py:66
  12.4 2.8 collective-permute-start.1
  23.1 3.7 collective-permute-done
  26.8 7.2 %negate_divide_fusion.1 = (f32[6,8,32,256]{3,0,2,1:T(8,128)S(1)}, f32[6,8,32,256]{3,0,2,1:T(8,128)S(1)}) fusion(f32[8,32,256]{2,1,0:T(8,128)S(1)} %get-tuple-element.18, f32[6,8,32,256]{3,0,2,1:T(8,128)S(1)} %bitcast.147, f32[6,1,32,256]{3,0,2,1:T(8,128)} %collective-permute-done.1, f32[6,1,32,256]{3,0,2,1:T(8,128)} %collective-permute-done, ...), kind=kOutput, calls=%fused_computation.119 | convolution fusion | flops 38141952 | bytes 14683136 | tf_op jit(solution)/shard_map/vw,wxyz->vxyz/dot_general | solution.py:25
  38.6 3.6 collective-permute-start.2
  45.2 4.0 collective-permute-done.2
  49.2 3.9 fusion.18
  57.7 3.9 collective-permute-start.4
  63.7 3.9 collective-permute-done.4
  67.6 4.9 fusion.14
  72.5 16.8 %copy.60 = f32[6,65536]{0,1:T(8,128)} copy(f32[6,65536]{1,0:T(8,128)S(1)} %bitcast.151) | data formatting | bytes 3145728 | tf_op jit(solution)/shard_map/reshape | solution.py:76
  89.3 118.8 %gather_fusion = f32[32768,6]{1,0:T(8,128)} fusion(f32[6,65536]{0,1:T(8,128)} %copy.60, s32[32768]{0:T(1024)S(1)} %broadcast_clamp_fusion), kind=kCustom, calls=%fused_computation | custom fusion | bytes 1703936 | tf_op jit(solution)/shard_map/gather | solution.py:77
  208.1 7.7 %multiply_reduce_fusion.1 = f32[16,2,128,6]{3,2,1,0:T(8,128)S(1)} fusion(f32[16,2,128,8,6]{4,2,3,1,0:T(8,128)} %bitcast.148, f32[16,2,128,8]{2,3,1,0:T(8,128)S(1)} %bitcast.152), kind=kLoop, calls=%fused_computation.5 | loop fusion | flops 368640 | bytes 1015808
  217.1 9.3 %all-to-all-start.1 = ((f32[6,16,2,128]{3,2,0,1:T(2,128)}), f32[6,16,2,128]{3,2,0,1:T(2,128)S(1)}, u32[]{:S(2)}, u32[]{:S(2)}) async-start(f32[6,16,2,128]{3,2,0,1:T(2,128)} %bitcast.37), calls=%async_computation.1 | async-start | bytes 196608 | tf_op jit(solution)/shard_map/all_to_all | solution.py:79
  226.5 8.4 %all-to-all-done.1 = f32[6,16,2,128]{3,2,0,1:T(2,128)S(1)} async-done(((f32[6,16,2,128]{3,2,0,1:T(2,128)}), f32[6,16,2,128]{3,2,0,1:T(2,128)S(1)}, u32[]{:S(2)}, u32[]{:S(2)}) %all-to-all-start.1) | async-done | bytes 98336 | tf_op jit(solution)/shard_map/all_to_all | solution.py:79
  235.7 32.3 %scatter_fusion = f32[6,65536]{0,1:T(8,128)} fusion(f32[6,65536]{0,1:T(8,128)} %copy.60, s32[4096]{0:T(1024)S(1)} %bitcast.164, f32[4096,6]{1,0:T(8,128)S(1)} %copy.61), kind=kCustom, calls=%fused_computation.2 | custom fusion | bytes 311296 | tf_op jit(solution)/shard_map/scatter | solution.py:81
  268.0 17.8 %copy.70 = f32[6,8,32,256]{3,0,2,1:T(8,128)S(1)} copy(f32[6,8,32,256]{0,3,2,1:T(8,128)} %bitcast.142) | data formatting | bytes 3145728 | tf_op jit(solution)/shard_map/reshape | solution.py:82
  290.5 3.6 collective-permute-start.6
  298.4 4.3 collective-permute-done.6
  302.8 5.8 %negate_divide_fusion = (f32[6,8,32,256]{3,0,2,1:T(8,128)S(1)}, f32[6,8,32,256]{3,0,2,1:T(8,128)S(1)}) fusion(f32[8,32,256]{2,1,0:T(8,128)S(1)} %get-tuple-element.18, f32[6,8,32,256]{3,0,2,1:T(8,128)S(1)} %copy.70, f32[6,1,32,256]{3,0,2,1:T(8,128)S(1)} %collective-permute-done.7, f32[6,1,32,256]{3,0,2,1:T(8,128)S(1)} %collective-permute-done.6, ...), kind=kOutput, calls=%fused_computation.91 | convolution fusion | flops 38141952 | bytes 16256000 | tf_op jit(solution)/shard_map/vw,wxyz->vxyz/dot_general | solution.py:25
  313.1 3.6 collective-permute-start.8
  320.3 4.0 collective-permute-done.8
  324.3 4.2 fusion.8
  333.2 3.6 collective-permute-start.10
  339.3 4.0 collective-permute-done.10
  343.4 5.8 %fusion.4 = f32[6,8,32,256]{3,0,2,1:T(8,128)} fusion(f32[6,8,32,256]{3,0,2,1:T(8,128)S(1)} %copy.70, f32[6,8,32,256]{3,0,2,1:T(8,128)S(1)} %get-tuple-element.25, f32[6,8,32,256]{3,0,2,1:T(8,128)S(1)} %fusion.8, f32[8,32,256,6]{2,3,1,0:T(8,128)S(1)} %fusion.22, f32[8,32,256,6]{2,3,1,0:T(8,128)S(1)} %fusion.25, ...), kind=kOutput, calls=%fused_computation.47 | convolution fusion | flops 37355520 | bytes 15993856 | tf_op jit(solution)/shard_map/vw,wxyz->vxyz/dot_general | solution.py:25
  349.2 16.4 %copy.73 = f32[6,65536]{0,1:T(8,128)} copy(f32[6,65536]{1,0:T(8,128)} %bitcast.150) | data formatting | bytes 3145728 | tf_op jit(solution)/shard_map/reshape | solution.py:76
  365.6 118.8 %gather_fusion.1 = f32[32768,6]{1,0:T(8,128)} fusion(f32[6,65536]{0,1:T(8,128)} %copy.73, s32[32768]{0:T(1024)S(1)} %broadcast_clamp_fusion), kind=kCustom, calls=%fused_computation.1 | custom fusion | bytes 1703936 | tf_op jit(solution)/shard_map/gather | solution.py:77
  484.4 7.7 %multiply_reduce_fusion = f32[16,2,128,6]{3,2,1,0:T(8,128)S(1)} fusion(f32[16,2,128,8,6]{4,2,3,1,0:T(8,128)} %bitcast.149, f32[16,2,128,8]{2,3,1,0:T(8,128)S(1)} %bitcast.153), kind=kLoop, calls=%fused_computation.4 | loop fusion | flops 368640 | bytes 1015808
  492.7 13.4 %all_to_all.15 = f32[6,16,2,128]{3,2,0,1:T(2,128)S(1)} all-to-all(f32[6,16,2,128]{3,2,0,1:T(2,128)S(1)} %bitcast.157), channel_id=1, replica_groups=mesh['comp'=16,'blk'=16] {'comp'}, dimensions={1} | all-to-all | bytes 196608 | tf_op jit(solution)/shard_map/all_to_all | solution.py:79
  506.9 32.2 %scatter_fusion.1 = f32[6,65536]{0,1:T(8,128)} fusion(f32[6,65536]{0,1:T(8,128)} %copy.73, s32[4096]{0:T(1024)S(1)} %bitcast.165, f32[4096,6]{1,0:T(8,128)S(1)} %copy.74), kind=kCustom, calls=%fused_computation.3 | custom fusion | bytes 311296 | tf_op jit(solution)/shard_map/scatter | solution.py:81
  539.1 20.5 %copy.75 = f32[1,6,8,32,256]{4,3,2,1,0:T(8,128)} copy(f32[1,6,8,32,256]{1,4,3,2,0:T(8,128)} %bitcast.143) | data formatting | bytes 3145728 | tf_op jit(solution)/shard_map/broadcast_in_dim;reshape | solution.py:83
  (69 shorter events, 52.7 us)
Async XLA Ops:
  0.0 17.7 %copy-start = (s32[1,16,16]{2,1,0:T(8,128)S(1)}, s32[1,16,16]{2,1,0:T(8,128)}, u32[]{:S(2)}) copy-start(s32[1,16,16]{2,1,0:T(8,128)} %param.15) | copy-start | bytes 3076
  0.0 208.1 %all-to-all-start = ((f32[16,2,8,128]{3,2,1,0:T(8,128)}), f32[16,2,8,128]{3,2,1,0:T(8,128)S(1)}, u32[]{:S(2)}, u32[]{:S(2)}) async-start(f32[16,2,8,128]{3,2,1,0:T(8,128)} %bitcast.167), calls=%async_computation | async-start | bytes 262144 | tf_op jit(solution)/shard_map/all_to_all | solution.py:66
  9.3 8.8 %copy-start.7 = (f32[1,3,6,6]{3,0,2,1:T(1,128)S(1)}, f32[1,3,6,6]{3,0,2,1:T(1,128)}, u32[]{:S(2)}) copy-start(f32[1,3,6,6]{3,0,2,1:T(1,128)} %param.11) | copy-start | bytes 1300
  9.3 8.8 %copy-start.5 = (s32[1,1,16,2,8,128]{5,4,3,2,1,0:T(8,128)S(1)}, s32[1,1,16,2,8,128]{5,4,3,2,1,0:T(8,128)}, u32[]{:S(2)}) copy-start(s32[1,1,16,2,8,128]{5,4,3,2,1,0:T(8,128)} %param.12) | copy-start | bytes 393220
  12.4 10.7 %collective-permute-start.1 = (f32[6,1,32,256]{3,0,2,1:T(8,128)}, f32[6,1,32,256]{3,0,2,1:T(8,128)}, u32[]{:S(2)}, u32[]{:S(2)}) collective-permute-start(f32[6,1,32,256]{3,0,2,1:T(8,128)} %get-tuple-element.15), channel_id=1, source_target_pairs={{0,1},{1,2},{2,3},{3,4},{4,5},{5,6},{6,7},{7,8},{8,9},{9,10},{10,1... | collective-permute-start | bytes 589832 | tf_op jit(solution)/shard_map/ppermute | solution.py:16
  15.2 11.6 %collective-permute-start = (f32[6,1,32,256]{3,0,2,1:T(8,128)S(1)}, f32[6,1,32,256]{3,0,2,1:T(8,128)}, u32[]{:S(2)}, u32[]{:S(2)}) collective-permute-start(f32[6,1,32,256]{3,0,2,1:T(8,128)S(1)} %get-tuple-element.16), channel_id=1, source_target_pairs={{1,0},{2,1},{3,2},{4,3},{5,4},{6,5},{7,6},{8,7},{9,8},{10,9},{11,1... | collective-permute-start | bytes 589832 | tf_op jit(solution)/shard_map/ppermute | solution.py:19
  21.0 2.1 copy-start.4
  21.0 5.9 %copy-start.8 = (f32[1,6,8,32,256]{4,3,2,1,0:T(8,128)S(1)}, f32[1,6,8,32,256]{4,3,2,1,0:T(8,128)}, u32[]{:S(2)}) copy-start(f32[1,6,8,32,256]{4,3,2,1,0:T(8,128)} %param.9) | copy-start | bytes 4718596
  36.7 8.5 %collective-permute-start.3 = (f32[6,1,32,256]{3,0,2,1:T(8,128)S(1)}, f32[6,1,32,256]{3,0,2,1:T(8,128)S(1)}, u32[]{:S(2)}, u32[]{:S(2)}) collective-permute-start(f32[6,1,32,256]{3,0,2,1:T(8,128)S(1)} %get-tuple-element.13), channel_id=1, source_target_pairs={{0,1},{1,2},{2,3},{3,4},{4,5},{5,6},{6,7},{7,8},{8,9},{9,10},{10,1... | collective-permute-start | bytes 589832 | tf_op jit(solution)/shard_map/ppermute | solution.py:16
  38.6 10.6 %collective-permute-start.2 = (f32[6,1,32,256]{3,0,2,1:T(8,128)S(1)}, f32[6,1,32,256]{3,0,2,1:T(8,128)S(1)}, u32[]{:S(2)}, u32[]{:S(2)}) collective-permute-start(f32[6,1,32,256]{3,0,2,1:T(8,128)S(1)} %get-tuple-element.14), channel_id=1, source_target_pairs={{1,0},{2,1},{3,2},{4,3},{5,4},{6,5},{7,6},{8,7},{9,8},{10,9},{11,1... | collective-permute-start | bytes 589832 | tf_op jit(solution)/shard_map/ppermute | solution.py:19
  55.8 7.9 %collective-permute-start.5 = (f32[6,1,32,256]{3,0,2,1:T(8,128)S(1)}, f32[6,1,32,256]{3,0,2,1:T(8,128)S(1)}, u32[]{:S(2)}, u32[]{:S(2)}) collective-permute-start(f32[6,1,32,256]{3,0,2,1:T(8,128)S(1)} %get-tuple-element.11), channel_id=1, source_target_pairs={{0,1},{1,2},{2,3},{3,4},{4,5},{5,6},{6,7},{7,8},{8,9},{9,10},{10,1... | collective-permute-start | bytes 589832 | tf_op jit(solution)/shard_map/ppermute | solution.py:16
  57.7 9.8 %copy-start.2 = (f32[1,6,8,32,256]{4,3,2,1,0:T(8,128)S(1)}, f32[1,6,8,32,256]{4,3,2,1,0:T(8,128)}, u32[]{:S(2)}) copy-start(f32[1,6,8,32,256]{4,3,2,1,0:T(8,128)} %param.8) | copy-start | bytes 4718596
  57.7 9.8 %collective-permute-start.4 = (f32[6,1,32,256]{3,0,2,1:T(8,128)S(1)}, f32[6,1,32,256]{3,0,2,1:T(8,128)S(1)}, u32[]{:S(2)}, u32[]{:S(2)}) collective-permute-start(f32[6,1,32,256]{3,0,2,1:T(8,128)S(1)} %get-tuple-element.12), channel_id=1, source_target_pairs={{1,0},{2,1},{3,2},{4,3},{5,4},{6,5},{7,6},{8,7},{9,8},{10,9},{11,1... | collective-permute-start | bytes 589832 | tf_op jit(solution)/shard_map/ppermute | solution.py:19
  215.8 10.6 %copy-start.6 = (s32[1,1,16,2,128]{4,3,2,1,0:T(2,128)S(1)}, s32[1,1,16,2,128]{4,3,2,1,0:T(2,128)}, u32[]{:S(2)}) copy-start(s32[1,1,16,2,128]{4,3,2,1,0:T(2,128)} %param.14) | copy-start | bytes 49156
  217.1 17.8 %all-to-all-start.1 = ((f32[6,16,2,128]{3,2,0,1:T(2,128)}), f32[6,16,2,128]{3,2,0,1:T(2,128)S(1)}, u32[]{:S(2)}, u32[]{:S(2)}) async-start(f32[6,16,2,128]{3,2,0,1:T(2,128)} %bitcast.37), calls=%async_computation.1 | async-start | bytes 196608 | tf_op jit(solution)/shard_map/all_to_all | solution.py:79
  288.5 9.9 %collective-permute-start.7 = (f32[6,1,32,256]{3,0,2,1:T(8,128)S(1)}, f32[6,1,32,256]{3,0,2,1:T(8,128)S(1)}, u32[]{:S(2)}, u32[]{:S(2)}) collective-permute-start(f32[6,1,32,256]{3,0,2,1:T(8,128)S(1)} %get-tuple-element.9), channel_id=1, source_target_pairs={{0,1},{1,2},{2,3},{3,4},{4,5},{5,6},{6,7},{7,8},{8,9},{9,10},{10,1... | collective-permute-start | bytes 589832 | tf_op jit(solution)/shard_map/ppermute | solution.py:16
  290.4 12.3 %copy-start.3 = (f32[1,6,8,32,256]{4,3,2,1,0:T(8,128)S(1)}, f32[1,6,8,32,256]{4,3,2,1,0:T(8,128)}, u32[]{:S(2)}) copy-start(f32[1,6,8,32,256]{4,3,2,1,0:T(8,128)} %param.8) | copy-start | bytes 4718596
  290.4 12.3 %copy-start.9 = (f32[1,6,8,32,256]{4,3,2,1,0:T(8,128)S(1)}, f32[1,6,8,32,256]{4,3,2,1,0:T(8,128)}, u32[]{:S(2)}) copy-start(f32[1,6,8,32,256]{4,3,2,1,0:T(8,128)} %param.9) | copy-start | bytes 4718596
  290.5 12.3 %collective-permute-start.6 = (f32[6,1,32,256]{3,0,2,1:T(8,128)S(1)}, f32[6,1,32,256]{3,0,2,1:T(8,128)S(1)}, u32[]{:S(2)}, u32[]{:S(2)}) collective-permute-start(f32[6,1,32,256]{3,0,2,1:T(8,128)S(1)} %get-tuple-element.10), channel_id=1, source_target_pairs={{1,0},{2,1},{3,2},{4,3},{5,4},{6,5},{7,6},{8,7},{9,8},{10,9},{11,1... | collective-permute-start | bytes 589832 | tf_op jit(solution)/shard_map/ppermute | solution.py:19
  311.2 9.0 %collective-permute-start.9 = (f32[6,1,32,256]{3,0,2,1:T(8,128)S(1)}, f32[6,1,32,256]{3,0,2,1:T(8,128)S(1)}, u32[]{:S(2)}, u32[]{:S(2)}) collective-permute-start(f32[6,1,32,256]{3,0,2,1:T(8,128)S(1)} %get-tuple-element.7), channel_id=1, source_target_pairs={{0,1},{1,2},{2,3},{3,4},{4,5},{5,6},{6,7},{7,8},{8,9},{9,10},{10,1... | collective-permute-start | bytes 589832 | tf_op jit(solution)/shard_map/ppermute | solution.py:16
  313.1 11.2 %collective-permute-start.8 = (f32[6,1,32,256]{3,0,2,1:T(8,128)S(1)}, f32[6,1,32,256]{3,0,2,1:T(8,128)S(1)}, u32[]{:S(2)}, u32[]{:S(2)}) collective-permute-start(f32[6,1,32,256]{3,0,2,1:T(8,128)S(1)} %get-tuple-element.8), channel_id=1, source_target_pairs={{1,0},{2,1},{3,2},{4,3},{5,4},{6,5},{7,6},{8,7},{9,8},{10,9},{11,1... | collective-permute-start | bytes 589832 | tf_op jit(solution)/shard_map/ppermute | solution.py:19
  331.2 8.1 %collective-permute-start.11 = (f32[6,1,32,256]{3,0,2,1:T(8,128)S(1)}, f32[6,1,32,256]{3,0,2,1:T(8,128)S(1)}, u32[]{:S(2)}, u32[]{:S(2)}) collective-permute-start(f32[6,1,32,256]{3,0,2,1:T(8,128)S(1)} %get-tuple-element.5), channel_id=1, source_target_pairs={{0,1},{1,2},{2,3},{3,4},{4,5},{5,6},{6,7},{7,8},{8,9},{9,10},{10,1... | collective-permute-start | bytes 589832 | tf_op jit(solution)/shard_map/ppermute | solution.py:16
  333.2 10.2 %collective-permute-start.10 = (f32[6,1,32,256]{3,0,2,1:T(8,128)S(1)}, f32[6,1,32,256]{3,0,2,1:T(8,128)S(1)}, u32[]{:S(2)}, u32[]{:S(2)}) collective-permute-start(f32[6,1,32,256]{3,0,2,1:T(8,128)S(1)} %get-tuple-element.6), channel_id=1, source_target_pairs={{1,0},{2,1},{3,2},{4,3},{5,4},{6,5},{7,6},{8,7},{9,8},{10,9},{11,1... | collective-permute-start | bytes 589832 | tf_op jit(solution)/shard_map/ppermute | solution.py:19
  539.1 20.5 %copy-start.1 = (s32[1,16,16]{2,1,0:T(8,128)S(1)}, s32[1,16,16]{2,1,0:T(8,128)}, u32[]{:S(2)}) copy-start(s32[1,16,16]{2,1,0:T(8,128)} %param.15) | copy-start | bytes 3076
where the time goes:
time: 570 us; the launch traced here: 560 us
  local copies, waits for them, and re-layouts  381 us (67%)
  matrix products  59.9 us (11%)
  starting transfers between devices  51.8 us (9%)
  waiting for transfers between devices  37.6 us (7%)
  other arithmetic  15.7 us (3%)
  blocking collectives  13.4 us (2%)
    gather x2, local copies, waits for them, and re-layouts, shards(): values = flat[:, corner_cell].reshape(nvar, comps, slots, 8, tile)  238 us
    scatter x2, local copies, waits for them, and re-layouts, shards(): flat = flat.at[:, target_cell].set(incoming, mode='drop')  64.5 us
    dot_general x18, matrix products, mix(): jnp.einsum('vw,wxyz->vxyz', jac_dim, field, precision=lax.Precision.HIGHEST)  59.9 us
    reshape x2, local copies, waits for them, and re-layouts, shards(): flat = state.reshape(nvar, total_cells)  33.2 us
    ppermute x6, waiting for transfers between devices, padded_2(): lax.ppermute(lax.slice_in_dim(block, 0, width, axis=dim), axis, backward)  24 us
    ppermute x6, starting transfers between devices, padded_2(): lax.ppermute(lax.slice_in_dim(block, 0, width, axis=dim), axis, backward)  20.8 us
    another operation x1, local copies, waits for them, and re-layouts, shards(): return state[None]  20.5 us
    reshape x1, local copies, waits for them, and re-layouts, shards(): state = flat.reshape(nvar, rows, width_y, width_z)  17.8 us
  transfers between devices with their start and end apart: 14, of which 11 were waited for; matrix products, arithmetic and copies ran while one was open for 31% of the time, Pallas kernels for 0%

commit v1 on v0

--- a/solution.py
+++ b/solution.py
@@ -76,7 +76,12 @@
         flat = state.reshape(nvar, total_cells)
         values = flat[:, corner_cell].reshape(nvar, comps, slots, 8, tile)
         packed = jnp.einsum("vcskp,cskp->vcsp", values, held, precision=lax.Precision.HIGHEST)
-        arrived = lax.all_to_all(packed, "comp", split_axis=1, concat_axis=1, tiled=True)
+        arrived = jnp.concatenate(
+            lax.all_to_all(
+                jnp.stack(jnp.split(packed, lax.axis_size("comp"), axis=1)), "comp", 0, 0
+            ),
+            axis=1,
+        )
         incoming = arrived.reshape(nvar, -1)
         flat = flat.at[:, target_cell].set(incoming, mode="drop")
         state = flat.reshape(nvar, rows, width_y, width_z)

time: 570 us -> 579 us (1.016)
  local copies, waits for them, and re-layouts: 381 us -> 390 us
    unnamed x21 -> x51, local copies, waits for them, and re-layouts: 2.41 us -> 11.4 us
where the time goes in v1:
time: 579 us; the launch traced here: 569 us
  local copies, waits for them, and re-layouts  390 us (67%)
  matrix products  59.9 us (10%)
  starting transfers between devices  51.8 us (9%)
  waiting for transfers between devices  37.6 us (6%)
  other arithmetic  15.7 us (3%)
  blocking collectives  13.4 us (2%)
    gather x2, local copies, waits for them, and re-layouts, shards(): values = flat[:, corner_cell].reshape(nvar, comps, slots, 8, tile)  238 us
    scatter x2, local copies, waits for them, and re-layouts, shards(): flat = flat.at[:, target_cell].set(incoming, mode='drop')  64.5 us
    dot_general x18, matrix products, mix(): jnp.einsum('vw,wxyz->vxyz', jac_dim, field, precision=lax.Precision.HIGHEST)  59.9 us
    reshape x2, local copies, waits for them, and re-layouts, shards(): flat = state.reshape(nvar, total_cells)  33.2 us
    ppermute x6, waiting for transfers between devices, padded_2(): lax.ppermute(lax.slice_in_dim(block, 0, width, axis=dim), axis, backward)  24 us
    ppermute x6, starting transfers between devices, padded_2(): lax.ppermute(lax.slice_in_dim(block, 0, width, axis=dim), axis, backward)  20.8 us
    another operation x1, local copies, waits for them, and re-layouts, shards(): return state[None]  20.5 us
    reshape x1, local copies, waits for them, and re-layouts, shards(): state = flat.reshape(nvar, rows, width_y, width_z)  17.8 us
  transfers between devices with their start and end apart: 14, of which 11 were waited for; matrix products, arithmetic and copies ran while one was open for 31% of the time, Pallas kernels for 0%

profile of v1, /device:TPU:27, one launch (start us, length us, event | category | flops | bytes accessed | tf_op | source)
XLA Modules:
  0.0 569.1 jit_solution(6221161298700552198)
XLA Ops:
  0.0 9.3 %all-to-all-start = ((f32[16,2,8,128]{3,2,1,0:T(8,128)}), f32[16,2,8,128]{3,2,1,0:T(8,128)S(1)}, u32[]{:S(2)}, u32[]{:S(2)}) async-start(f32[16,2,8,128]{3,2,1,0:T(8,128)} %bitcast.394), calls=%async_computation | async-start | bytes 262144 | tf_op jit(solution)/shard_map/all_to_all | solution.py:66
  12.4 2.8 collective-permute-start.1
  23.1 3.7 collective-permute-done
  26.8 7.2 %negate_divide_fusion.1 = (f32[6,8,32,256]{3,0,2,1:T(8,128)S(1)}, f32[6,8,32,256]{3,0,2,1:T(8,128)S(1)}) fusion(f32[8,32,256]{2,1,0:T(8,128)S(1)} %get-tuple-element.18, f32[6,8,32,256]{3,0,2,1:T(8,128)S(1)} %bitcast.341, f32[6,1,32,256]{3,0,2,1:T(8,128)} %collective-permute-done.1, f32[6,1,32,256]{3,0,2,1:T(8,128)} %collective-permute-done, ...), kind=kOutput, calls=%fused_computation.119 | convolution fusion | flops 38141952 | bytes 14683136 | tf_op jit(solution)/shard_map/vw,wxyz->vxyz/dot_general | solution.py:25
  38.6 3.6 collective-permute-start.2
  45.2 4.0 collective-permute-done.2
  49.2 3.9 fusion.18
  57.7 3.9 collective-permute-start.4
  63.7 3.9 collective-permute-done.4
  67.6 4.9 fusion.14
  72.5 16.8 %copy.222 = f32[6,65536]{0,1:T(8,128)} copy(f32[6,65536]{1,0:T(8,128)S(1)} %bitcast.345) | data formatting | bytes 3145728 | tf_op jit(solution)/shard_map/reshape | solution.py:76
  89.3 118.8 %gather_fusion = f32[32768,6]{1,0:T(8,128)} fusion(f32[6,65536]{0,1:T(8,128)} %copy.222, s32[32768]{0:T(1024)S(1)} %broadcast_clamp_fusion), kind=kCustom, calls=%fused_computation | custom fusion | bytes 1703936 | tf_op jit(solution)/shard_map/gather | solution.py:77
  208.1 7.7 %multiply_reduce_fusion.1 = f32[16,2,128,6]{3,2,1,0:T(8,128)S(1)} fusion(f32[16,2,128,8,6]{4,2,3,1,0:T(8,128)} %bitcast.342, f32[16,2,128,8]{2,3,1,0:T(8,128)S(1)} %bitcast.346), kind=kLoop, calls=%fused_computation.5 | loop fusion | flops 368640 | bytes 1015808
  226.0 9.3 %all-to-all-start.1 = ((f32[16,6,1,2,128]{4,3,2,1,0:T(2,128)}), f32[16,6,1,2,128]{4,3,2,1,0:T(2,128)S(1)}, u32[]{:S(2)}, u32[]{:S(2)}) async-start(f32[16,6,1,2,128]{4,3,2,1,0:T(2,128)} %constant_dynamic-update-slice_fusion), calls=%async_computation.1 | async-start | bytes 196608 | tf_op jit(solution)/shard_map/all_to_all | solution.py:80
  235.4 8.4 %all-to-all-done.1 = f32[16,6,1,2,128]{4,3,2,1,0:T(2,128)S(1)} async-done(((f32[16,6,1,2,128]{4,3,2,1,0:T(2,128)}), f32[16,6,1,2,128]{4,3,2,1,0:T(2,128)S(1)}, u32[]{:S(2)}, u32[]{:S(2)}) %all-to-all-start.1) | async-done | bytes 98336 | tf_op jit(solution)/shard_map/all_to_all | solution.py:80
  244.6 32.3 %scatter_fusion = f32[6,65536]{0,1:T(8,128)} fusion(f32[6,65536]{0,1:T(8,128)} %copy.222, s32[4096]{0:T(1024)S(1)} %bitcast.391, f32[4096,6]{1,0:T(8,128)S(1)} %copy.223), kind=kCustom, calls=%fused_computation.2 | custom fusion | bytes 311296 | tf_op jit(solution)/shard_map/scatter | solution.py:86
  276.9 17.8 %copy.232 = f32[6,8,32,256]{3,0,2,1:T(8,128)S(1)} copy(f32[6,8,32,256]{0,3,2,1:T(8,128)} %bitcast.336) | data formatting | bytes 3145728 | tf_op jit(solution)/shard_map/reshape | solution.py:87
  299.3 3.6 collective-permute-start.6
  307.3 4.3 collective-permute-done.6
  311.6 5.8 %negate_divide_fusion = (f32[6,8,32,256]{3,0,2,1:T(8,128)S(1)}, f32[6,8,32,256]{3,0,2,1:T(8,128)S(1)}) fusion(f32[8,32,256]{2,1,0:T(8,128)S(1)} %get-tuple-element.18, f32[6,8,32,256]{3,0,2,1:T(8,128)S(1)} %copy.232, f32[6,1,32,256]{3,0,2,1:T(8,128)S(1)} %collective-permute-done.7, f32[6,1,32,256]{3,0,2,1:T(8,128)S(1)} %collective-permute-done.6, ...), kind=kOutput, calls=%fused_computation.91 | convolution fusion | flops 38141952 | bytes 16256000 | tf_op jit(solution)/shard_map/vw,wxyz->vxyz/dot_general | solution.py:25
  322.0 3.6 collective-permute-start.8
  329.1 4.0 collective-permute-done.8
  333.2 4.2 fusion.8
  342.0 3.6 collective-permute-start.10
  348.2 4.0 collective-permute-done.10
  352.3 5.8 %fusion.4 = f32[6,8,32,256]{3,0,2,1:T(8,128)} fusion(f32[6,8,32,256]{3,0,2,1:T(8,128)S(1)} %copy.232, f32[6,8,32,256]{3,0,2,1:T(8,128)S(1)} %get-tuple-element.25, f32[6,8,32,256]{3,0,2,1:T(8,128)S(1)} %fusion.8, f32[8,32,256,6]{2,3,1,0:T(8,128)S(1)} %fusion.22, f32[8,32,256,6]{2,3,1,0:T(8,128)S(1)} %fusion.25, ...), kind=kOutput, calls=%fused_computation.47 | convolution fusion | flops 37355520 | bytes 15993856 | tf_op jit(solution)/shard_map/vw,wxyz->vxyz/dot_general | solution.py:25
  358.1 16.4 %copy.250 = f32[6,65536]{0,1:T(8,128)} copy(f32[6,65536]{1,0:T(8,128)} %bitcast.344) | data formatting | bytes 3145728 | tf_op jit(solution)/shard_map/reshape | solution.py:76
  374.5 118.8 %gather_fusion.1 = f32[32768,6]{1,0:T(8,128)} fusion(f32[6,65536]{0,1:T(8,128)} %copy.250, s32[32768]{0:T(1024)S(1)} %broadcast_clamp_fusion), kind=kCustom, calls=%fused_computation.1 | custom fusion | bytes 1703936 | tf_op jit(solution)/shard_map/gather | solution.py:77
  493.3 7.7 %multiply_reduce_fusion = f32[16,2,128,6]{3,2,1,0:T(8,128)S(1)} fusion(f32[16,2,128,8,6]{4,2,3,1,0:T(8,128)} %bitcast.343, f32[16,2,128,8]{2,3,1,0:T(8,128)S(1)} %bitcast.347), kind=kLoop, calls=%fused_computation.4 | loop fusion | flops 368640 | bytes 1015808
  501.8 13.4 %all_to_all.15 = f32[16,6,1,2,128]{4,3,2,1,0:T(2,128)S(1)} all-to-all(f32[16,6,1,2,128]{4,3,2,1,0:T(2,128)S(1)} %constant_dynamic-update-slice_fusion.16), channel_id=1, replica_groups=mesh['comp'=16,'blk'=16] {'comp'}, dimensions={0} | all-to-all | bytes 196608 | tf_op jit(solution)/shard_map/all_to_all | solution.py:80
  516.0 32.2 %scatter_fusion.1 = f32[6,65536]{0,1:T(8,128)} fusion(f32[6,65536]{0,1:T(8,128)} %copy.250, s32[4096]{0:T(1024)S(1)} %bitcast.392, f32[4096,6]{1,0:T(8,128)S(1)} %copy.251), kind=kCustom, calls=%fused_computation.3 | custom fusion | bytes 311296 | tf_op jit(solution)/shard_map/scatter | solution.py:86
  548.2 20.5 %copy.252 = f32[1,6,8,32,256]{4,3,2,1,0:T(8,128)} copy(f32[1,6,8,32,256]{1,4,3,2,0:T(8,128)} %bitcast.337) | data formatting | bytes 3145728 | tf_op jit(solution)/shard_map/broadcast_in_dim;reshape | solution.py:88
  (101 shorter events, 61.7 us)
Async XLA Ops:
  0.0 17.7 %copy-start = (s32[1,16,16]{2,1,0:T(8,128)S(1)}, s32[1,16,16]{2,1,0:T(8,128)}, u32[]{:S(2)}) copy-start(s32[1,16,16]{2,1,0:T(8,128)} %param.15) | copy-start | bytes 3076
  0.0 208.1 %all-to-all-start = ((f32[16,2,8,128]{3,2,1,0:T(8,128)}), f32[16,2,8,128]{3,2,1,0:T(8,128)S(1)}, u32[]{:S(2)}, u32[]{:S(2)}) async-start(f32[16,2,8,128]{3,2,1,0:T(8,128)} %bitcast.394), calls=%async_computation | async-start | bytes 262144 | tf_op jit(solution)/shard_map/all_to_all | solution.py:66
  9.3 8.8 %copy-start.7 = (f32[1,3,6,6]{3,0,2,1:T(1,128)S(1)}, f32[1,3,6,6]{3,0,2,1:T(1,128)}, u32[]{:S(2)}) copy-start(f32[1,3,6,6]{3,0,2,1:T(1,128)} %param.11) | copy-start | bytes 1300
  9.3 8.8 %copy-start.5 = (s32[1,1,16,2,8,128]{5,4,3,2,1,0:T(8,128)S(1)}, s32[1,1,16,2,8,128]{5,4,3,2,1,0:T(8,128)}, u32[]{:S(2)}) copy-start(s32[1,1,16,2,8,128]{5,4,3,2,1,0:T(8,128)} %param.12) | copy-start | bytes 393220
  12.4 10.7 %collective-permute-start.1 = (f32[6,1,32,256]{3,0,2,1:T(8,128)}, f32[6,1,32,256]{3,0,2,1:T(8,128)}, u32[]{:S(2)}, u32[]{:S(2)}) collective-permute-start(f32[6,1,32,256]{3,0,2,1:T(8,128)} %get-tuple-element.15), channel_id=1, source_target_pairs={{0,1},{1,2},{2,3},{3,4},{4,5},{5,6},{6,7},{7,8},{8,9},{9,10},{10,1... | collective-permute-start | bytes 589832 | tf_op jit(solution)/shard_map/ppermute | solution.py:16
  15.2 11.6 %collective-permute-start = (f32[6,1,32,256]{3,0,2,1:T(8,128)S(1)}, f32[6,1,32,256]{3,0,2,1:T(8,128)}, u32[]{:S(2)}, u32[]{:S(2)}) collective-permute-start(f32[6,1,32,256]{3,0,2,1:T(8,128)S(1)} %get-tuple-element.16), channel_id=1, source_target_pairs={{1,0},{2,1},{3,2},{4,3},{5,4},{6,5},{7,6},{8,7},{9,8},{10,9},{11,1... | collective-permute-start | bytes 589832 | tf_op jit(solution)/shard_map/ppermute | solution.py:19
  21.0 2.1 copy-start.4
  21.0 5.9 %copy-start.8 = (f32[1,6,8,32,256]{4,3,2,1,0:T(8,128)S(1)}, f32[1,6,8,32,256]{4,3,2,1,0:T(8,128)}, u32[]{:S(2)}) copy-start(f32[1,6,8,32,256]{4,3,2,1,0:T(8,128)} %param.9) | copy-start | bytes 4718596
  36.7 8.5 %collective-permute-start.3 = (f32[6,1,32,256]{3,0,2,1:T(8,128)S(1)}, f32[6,1,32,256]{3,0,2,1:T(8,128)S(1)}, u32[]{:S(2)}, u32[]{:S(2)}) collective-permute-start(f32[6,1,32,256]{3,0,2,1:T(8,128)S(1)} %get-tuple-element.13), channel_id=1, source_target_pairs={{0,1},{1,2},{2,3},{3,4},{4,5},{5,6},{6,7},{7,8},{8,9},{9,10},{10,1... | collective-permute-start | bytes 589832 | tf_op jit(solution)/shard_map/ppermute | solution.py:16
  38.6 10.6 %collective-permute-start.2 = (f32[6,1,32,256]{3,0,2,1:T(8,128)S(1)}, f32[6,1,32,256]{3,0,2,1:T(8,128)S(1)}, u32[]{:S(2)}, u32[]{:S(2)}) collective-permute-start(f32[6,1,32,256]{3,0,2,1:T(8,128)S(1)} %get-tuple-element.14), channel_id=1, source_target_pairs={{1,0},{2,1},{3,2},{4,3},{5,4},{6,5},{7,6},{8,7},{9,8},{10,9},{11,1... | collective-permute-start | bytes 589832 | tf_op jit(solution)/shard_map/ppermute | solution.py:19
  55.8 7.9 %collective-permute-start.5 = (f32[6,1,32,256]{3,0,2,1:T(8,128)S(1)}, f32[6,1,32,256]{3,0,2,1:T(8,128)S(1)}, u32[]{:S(2)}, u32[]{:S(2)}) collective-permute-start(f32[6,1,32,256]{3,0,2,1:T(8,128)S(1)} %get-tuple-element.11), channel_id=1, source_target_pairs={{0,1},{1,2},{2,3},{3,4},{4,5},{5,6},{6,7},{7,8},{8,9},{9,10},{10,1... | collective-permute-start | bytes 589832 | tf_op jit(solution)/shard_map/ppermute | solution.py:16
  57.7 9.8 %copy-start.2 = (f32[1,6,8,32,256]{4,3,2,1,0:T(8,128)S(1)}, f32[1,6,8,32,256]{4,3,2,1,0:T(8,128)}, u32[]{:S(2)}) copy-start(f32[1,6,8,32,256]{4,3,2,1,0:T(8,128)} %param.8) | copy-start | bytes 4718596
  57.7 9.8 %collective-permute-start.4 = (f32[6,1,32,256]{3,0,2,1:T(8,128)S(1)}, f32[6,1,32,256]{3,0,2,1:T(8,128)S(1)}, u32[]{:S(2)}, u32[]{:S(2)}) collective-permute-start(f32[6,1,32,256]{3,0,2,1:T(8,128)S(1)} %get-tuple-element.12), channel_id=1, source_target_pairs={{1,0},{2,1},{3,2},{4,3},{5,4},{6,5},{7,6},{8,7},{9,8},{10,9},{11,1... | collective-permute-start | bytes 589832 | tf_op jit(solution)/shard_map/ppermute | solution.py:19
  215.8 19.5 %copy-start.6 = (s32[1,1,16,2,128]{4,3,2,1,0:T(2,128)S(1)}, s32[1,1,16,2,128]{4,3,2,1,0:T(2,128)}, u32[]{:S(2)}) copy-start(s32[1,1,16,2,128]{4,3,2,1,0:T(2,128)} %param.14) | copy-start | bytes 49156
  226.0 17.8 %all-to-all-start.1 = ((f32[16,6,1,2,128]{4,3,2,1,0:T(2,128)}), f32[16,6,1,2,128]{4,3,2,1,0:T(2,128)S(1)}, u32[]{:S(2)}, u32[]{:S(2)}) async-start(f32[16,6,1,2,128]{4,3,2,1,0:T(2,128)} %constant_dynamic-update-slice_fusion), calls=%async_computation.1 | async-start | bytes 196608 | tf_op jit(solution)/shard_map/all_to_all | solution.py:80
  297.4 9.9 %collective-permute-start.7 = (f32[6,1,32,256]{3,0,2,1:T(8,128)S(1)}, f32[6,1,32,256]{3,0,2,1:T(8,128)S(1)}, u32[]{:S(2)}, u32[]{:S(2)}) collective-permute-start(f32[6,1,32,256]{3,0,2,1:T(8,128)S(1)} %get-tuple-element.9), channel_id=1, source_target_pairs={{0,1},{1,2},{2,3},{3,4},{4,5},{5,6},{6,7},{7,8},{8,9},{9,10},{10,1... | collective-permute-start | bytes 589832 | tf_op jit(solution)/shard_map/ppermute | solution.py:16
  299.3 12.3 %copy-start.3 = (f32[1,6,8,32,256]{4,3,2,1,0:T(8,128)S(1)}, f32[1,6,8,32,256]{4,3,2,1,0:T(8,128)}, u32[]{:S(2)}) copy-start(f32[1,6,8,32,256]{4,3,2,1,0:T(8,128)} %param.8) | copy-start | bytes 4718596
  299.3 12.3 %copy-start.9 = (f32[1,6,8,32,256]{4,3,2,1,0:T(8,128)S(1)}, f32[1,6,8,32,256]{4,3,2,1,0:T(8,128)}, u32[]{:S(2)}) copy-start(f32[1,6,8,32,256]{4,3,2,1,0:T(8,128)} %param.9) | copy-start | bytes 4718596
  299.3 12.3 %collective-permute-start.6 = (f32[6,1,32,256]{3,0,2,1:T(8,128)S(1)}, f32[6,1,32,256]{3,0,2,1:T(8,128)S(1)}, u32[]{:S(2)}, u32[]{:S(2)}) collective-permute-start(f32[6,1,32,256]{3,0,2,1:T(8,128)S(1)} %get-tuple-element.10), channel_id=1, source_target_pairs={{1,0},{2,1},{3,2},{4,3},{5,4},{6,5},{7,6},{8,7},{9,8},{10,9},{11,1... | collective-permute-start | bytes 589832 | tf_op jit(solution)/shard_map/ppermute | solution.py:19
  320.1 9.0 %collective-permute-start.9 = (f32[6,1,32,256]{3,0,2,1:T(8,128)S(1)}, f32[6,1,32,256]{3,0,2,1:T(8,128)S(1)}, u32[]{:S(2)}, u32[]{:S(2)}) collective-permute-start(f32[6,1,32,256]{3,0,2,1:T(8,128)S(1)} %get-tuple-element.7), channel_id=1, source_target_pairs={{0,1},{1,2},{2,3},{3,4},{4,5},{5,6},{6,7},{7,8},{8,9},{9,10},{10,1... | collective-permute-start | bytes 589832 | tf_op jit(solution)/shard_map/ppermute | solution.py:16
  322.0 11.2 %collective-permute-start.8 = (f32[6,1,32,256]{3,0,2,1:T(8,128)S(1)}, f32[6,1,32,256]{3,0,2,1:T(8,128)S(1)}, u32[]{:S(2)}, u32[]{:S(2)}) collective-permute-start(f32[6,1,32,256]{3,0,2,1:T(8,128)S(1)} %get-tuple-element.8), channel_id=1, source_target_pairs={{1,0},{2,1},{3,2},{4,3},{5,4},{6,5},{7,6},{8,7},{9,8},{10,9},{11,1... | collective-permute-start | bytes 589832 | tf_op jit(solution)/shard_map/ppermute | solution.py:19
  340.1 8.1 %collective-permute-start.11 = (f32[6,1,32,256]{3,0,2,1:T(8,128)S(1)}, f32[6,1,32,256]{3,0,2,1:T(8,128)S(1)}, u32[]{:S(2)}, u32[]{:S(2)}) collective-permute-start(f32[6,1,32,256]{3,0,2,1:T(8,128)S(1)} %get-tuple-element.5), channel_id=1, source_target_pairs={{0,1},{1,2},{2,3},{3,4},{4,5},{5,6},{6,7},{7,8},{8,9},{9,10},{10,1... | collective-permute-start | bytes 589832 | tf_op jit(solution)/shard_map/ppermute | solution.py:16
  342.0 10.2 %collective-permute-start.10 = (f32[6,1,32,256]{3,0,2,1:T(8,128)S(1)}, f32[6,1,32,256]{3,0,2,1:T(8,128)S(1)}, u32[]{:S(2)}, u32[]{:S(2)}) collective-permute-start(f32[6,1,32,256]{3,0,2,1:T(8,128)S(1)} %get-tuple-element.6), channel_id=1, source_target_pairs={{1,0},{2,1},{3,2},{4,3},{5,4},{6,5},{7,6},{8,7},{9,8},{10,9},{11,1... | collective-permute-start | bytes 589832 | tf_op jit(solution)/shard_map/ppermute | solution.py:19
  548.2 20.5 %copy-start.1 = (s32[1,16,16]{2,1,0:T(8,128)S(1)}, s32[1,16,16]{2,1,0:T(8,128)}, u32[]{:S(2)}) copy-start(s32[1,16,16]{2,1,0:T(8,128)} %param.15) | copy-start | bytes 3076
